TPU v7x, 32 devices: a whole 2x2x4 slice. The times are simulated.
32 devices in a mesh: groups: 2 (over x), seq: 4 (over y, core), chan: 4 (over z).
Axes of the slice: x: 2, y: 2, z: 4, core: 2. Of those that a mesh axis runs over, the one named last changes fastest.
Arguments:
- dna_act: bfloat16 [6, 2048, 1280], P('groups', 'seq', 'chan'), parts along dimension 0, may hold values from -5 to 5
- conv_weight: bfloat16 [5, 1280, 1536], P(None, 'chan'), may hold values from -0.078125 to 0.078125
- head_weight: bfloat16 [7611, 1536], P(None, 'chan'), may hold values from -0.078125 to 0.078125
- track_ids: int32 [1024], P('groups'), parts along dimension 0, may hold values from 0 to 7610, as said below
- bin_mask: int32 [6, 1024], P('groups', ('seq', 'chan')), parts along dimension 0, may hold values 0 or 1
- counts: int32 [6, 1024, 512], P('groups', ('seq', 'chan')), parts along dimension 0, may hold values from 0 to 3
Outputs:
- grad_input: bfloat16 [6, 2048, 1280], P('groups', 'seq', 'chan'), parts along dimension 0
- grad_conv: float32 [10, 1280, 1536], P('groups', 'chan', 'seq'), parts along dimension 0
- grad_tracks: float32 [1024, 1536], P(('groups', 'seq'), 'chan'), parts along dimension 0
There are 2 independent parts, one for each index of `groups`. A program takes and returns all parts, laid end to end along the dimension named above; an argument that names none is the same for every part. Nothing has to cross between parts.
Inputs may be any that keep to these rules, and one draw needn't show every extreme that they name: `track_ids`: the 512 track numbers are distinct.
All inputs are finite; a program needn't handle non-finite values. No bound on the sum of `bin_mask` on one device may be relied on, other than what follows from the above.
Results may differ from a plain program's by a relative error of at most 0.011.
Values may be sent and summed in bfloat16 or wider, within the bound.
No kernel may reach another device: no remote copies, remote signals or barrier semaphores. Data moves between devices by JAX's collectives and lax.ppermute only.
A program may use at most 128 MiB of HBM per device.

v0:
```python
import jax
import jax.numpy as jnp
from jax import lax
from jax.sharding import PartitionSpec as P

KSIZE = 5


def padded_2(cells, sides, width):
    for axis, dim in sides:
        count = lax.axis_size(axis)
        ends = count - 1
        head = lax.slice_in_dim(cells, 0, width, axis=dim)
        tail = lax.slice_in_dim(cells, cells.shape[dim] - width, cells.shape[dim], axis=dim)
        cells = jnp.concatenate(
            [
                lax.ppermute(tail, axis, [(i, (i + 1) % count) for i in range(ends)]),
                cells,
                lax.ppermute(head, axis, [((i + 1) % count, i) for i in range(ends)]),
            ],
            axis=dim,
        )
    return cells


def exact_gelu(values):
    return jax.nn.gelu(values, approximate=False)


def local(dna_act, conv_weight, head_weight, track_ids, bin_mask, counts):
    seq_count, positions, channels = dna_act.shape
    out_width = conv_weight.shape[2]
    gelu_out, gelu_back = jax.vjp(exact_gelu, dna_act.astype(jnp.float32))
    activated = gelu_out.astype(jnp.bfloat16)
    padded = padded_2(activated, (("seq", 1),), 2)
    windows = jnp.concatenate(
        [padded[:, offset : offset + positions] for offset in range(KSIZE)], axis=2
    )
    flat_weight = conv_weight.reshape(KSIZE * channels, out_width)
    conv_part = jnp.einsum("stj,jo->sto", windows, flat_weight, preferred_element_type=jnp.float32)
    pooled_part = conv_part.reshape(seq_count, positions // 2, 2, out_width).sum(axis=2) * 0.5
    bin_rows = lax.psum_scatter(
        pooled_part.astype(jnp.bfloat16), "chan", scatter_dimension=1, tiled=True
    )
    local_rows = jnp.take(head_weight, track_ids, axis=0)
    chosen = lax.all_gather(local_rows, "chan", axis=1, tiled=True)
    logits = jnp.einsum("snd,md->snm", bin_rows, chosen, preferred_element_type=jnp.float32)
    mask_column = bin_mask.astype(jnp.float32)[:, :, None]
    grad_logit = (mask_column * (jnp.exp(logits) - counts.astype(jnp.float32))).astype(jnp.bfloat16)
    grad_bins = jnp.einsum(
        "snm,md->snd", grad_logit, chosen, preferred_element_type=jnp.float32
    ).astype(jnp.bfloat16)
    slab_grad = lax.all_gather(grad_bins, "chan", axis=1, tiled=True)
    track_part = jnp.einsum("snm,snd->md", grad_logit, bin_rows, preferred_element_type=jnp.float32)
    track_summed = lax.psum_scatter(
        track_part.astype(jnp.bfloat16), "seq", scatter_dimension=0, tiled=True
    )
    grad_tracks = lax.psum_scatter(track_summed, "chan", scatter_dimension=1, tiled=True).astype(
        jnp.float32
    )
    rim_grad = padded_2(slab_grad, (("seq", 1),), 1)
    wide_grad = jnp.repeat(rim_grad, 2, axis=1) * 0.5
    projected = jnp.einsum(
        "sqo,jo->sqj", wide_grad, flat_weight, preferred_element_type=jnp.float32
    )
    projected = projected.reshape(seq_count, positions + 4, KSIZE, channels)
    grad_acts = projected[:, 4 : 4 + positions, 0]
    for offset in range(1, KSIZE):
        grad_acts = grad_acts + projected[:, 4 - offset : 4 - offset + positions, offset]
    grad_input = gelu_back(grad_acts)[0].astype(jnp.bfloat16)
    slab_upsampled = jnp.repeat(slab_grad, 2, axis=1) * 0.5
    flat_grad = jnp.einsum(
        "stj,sto->jo", windows, slab_upsampled, preferred_element_type=jnp.float32
    )
    grad_conv = lax.psum_scatter(
        flat_grad.reshape(KSIZE, channels, out_width).astype(jnp.bfloat16),
        "seq",
        scatter_dimension=2,
        tiled=True,
    ).astype(jnp.float32)
    return (grad_input, grad_conv, grad_tracks)


def solution(mesh):
    in_specs = (
        P("groups", "seq", "chan"),
        P(None, "chan", None),
        P(None, "chan"),
        P("groups"),
        P("groups", ("seq", "chan")),
        P("groups", ("seq", "chan"), None),
    )
    out_specs = (
        P("groups", "seq", "chan"),
        P("groups", "chan", "seq"),
        P(("groups", "seq"), "chan"),
    )
    return jax.shard_map(local, mesh=mesh, in_specs=in_specs, out_specs=out_specs, check_vma=False)
```

profile of v0, /device:TPU:0, one launch (start us, length us, event | category | flops | bytes accessed | tf_op | source)
XLA Modules:
  0.0 317.8 jit_solution(13602244970949401829)
XLA Ops:
  8.9 6.0 %fusion.12 = (bf16[3,512,320]{2,1,0:T(8,128)(2,1)S(1)}, f32[3,512,320]{2,1,0:T(8,128)}) fusion(bf16[3,512,320]{2,1,0:T(8,128)(2,1)S(1)} %copy.17), kind=kLoop, calls=%fused_computation.19 | loop fusion | flops 32440320 | bytes 3932160 | tf_op jit(solution)/shard_map/convert_element_type | solution.py:34
  15.0 2.4 collective-permute-start
  18.7 5.2 %gather_fusion = bf16[512,384]{1,0:T(8,128)(2,1)S(1)} fusion(bf16[7611,384]{1,0:T(8,128)(2,1)} %param.8, s32[1024]{0:T(1024)S(1)} %pad_clamp_fusion), kind=kCustom, calls=%fused_computation | custom fusion | bytes 788480 | tf_op jit(solution)/shard_map/jit(_take)/gather | solution.py:45
  24.9 3.4 %pad_maximum_fusion = (bf16[3,512,320]{2,1,0:T(8,128)(2,1)S(1)}, bf16[3,512,320]{2,1,0:T(8,128)(2,1)}, bf16[3,512,320]{2,1,0:T(8,128)(2,1)}, bf16[3,512,320]{2,1,0:T(8,128)(2,1)}) fusion(bf16[3,2,320]{2,1,0:T(2,128)(2,1)S(1)} %collective-permute-done.1, bf16[3,512,320]{2,1,0:T(8,128)(2,1)S(1)} %get-tuple-element.12, ...), kind=kLoop, calls=%fused_computation.71 | loop fusion | flops 7864320 | bytes 4922880 | tf_op jit(solution)/shard_map/concatenate | solution.py:15
  28.3 9.0 %concatenate.17 = bf16[3,512,1600]{2,1,0:T(8,128)(2,1)} concatenate(bf16[3,512,320]{2,1,0:T(8,128)(2,1)} %get-tuple-element.20, bf16[3,512,320]{2,1,0:T(8,128)(2,1)} %get-tuple-element.21, bf16[3,512,320]{2,1,0:T(8,128)(2,1)S(1)} %get-tuple-element.12, bf16[3,512,320]{2,1,0:T(8,128)(2,1)} %get-tuple-element.17, bf16[3,512,320]{2,1,0:T(8,128)(2,1)S(1)} %get-tuple-element.16), dimensions={2} | concatenate | bytes 9830400 | tf_op jit(solution)/shard_map/concatenate | solution.py:36
  37.3 11.0 %dot_general.24 = bf16[3,256,2,1600]{3,2,1,0:T(2,128)(2,1)} reshape(bf16[3,512,1600]{2,1,0:T(8,128)(2,1)} %concatenate.17) | data formatting | bytes 9830400 | tf_op jit(solution)/shard_map/stj,jo->sto/dot_general | solution.py:40
  48.3 12.4 %fusion.7 = f32[3,256,1536]{2,1,0:T(8,128)S(1)} fusion(bf16[1600,1536,1,1]{1,0,3,2:T(8,128)(2,1)} %bitcast.55, bf16[3,256,2,1600]{3,2,1,0:T(2,128)(2,1)} %dot_general.24), kind=kOutput, calls=%fused_computation.14 | convolution fusion | flops 7550926848 | bytes 14548992 | tf_op jit(solution)/shard_map/stj,jo->sto/dot_general | solution.py:40
  60.7 2.1 multiply_convert_fusion
  63.5 2.7 all-gather.3.cloned.1.call-done
  66.2 49.4 %reduce-scatter.9.cloned.1.call-done = bf16[3,64,1536]{2,1,0:T(8,128)(2,1)} async-done(((bf16[3,256,1536]{2,1,0:T(8,128)(2,1)}), bf16[3,64,1536]{2,1,0:T(8,128)(2,1)}) %reduce-scatter.9.cloned.1.call-update) | async-done | bytes 589840 | tf_op jit(solution)/shard_map/reduce_scatter | solution.py:42
  115.6 2.3 fusion.62
  119.8 2.7 convolution_convert_fusion
  122.7 7.8 %copy.19 = bf16[1600,3,512]{2,0,1:T(8,128)(2,1)} copy(bf16[1600,3,512]{0,2,1:T(8,128)(2,1)} %bitcast.49) | data formatting | bytes 9830400 | tf_op jit(solution)/shard_map/stj,sto->jo/dot_general | solution.py:72
  130.5 16.8 %reduce-scatter.11.cloned.1.call-done = bf16[128,1536]{1,0:T(8,128)(2,1)} async-done(((bf16[512,1536]{1,0:T(8,128)(2,1)}), bf16[128,1536]{1,0:T(8,128)(2,1)}) %reduce-scatter.11.cloned.1.call-update) | async-done | bytes 393232 | tf_op jit(solution)/shard_map/reduce_scatter | solution.py:55
  147.3 1.9 copy.26
  149.3 50.0 %all-gather.5.cloned.1.call-done = bf16[3,256,1536]{2,1,0:T(8,128)(2,1)} async-done(((bf16[3,64,1536]{2,1,0:T(8,128)(2,1)}), bf16[3,256,1536]{2,1,0:T(8,128)(2,1)}) %all-gather.5.cloned.1.call-update) | async-done | bytes 2359312 | tf_op jit(solution)/shard_map/all_gather | solution.py:53
  199.3 1.9 broadcast_multiply_fusion
  201.2 4.0 %broadcast_in_dim.23 = bf16[3,256,2,1536]{3,2,1,0:T(2,128)(2,1)} broadcast(bf16[3,256,1536]{2,1,0:T(8,128)(2,1)S(1)} %broadcast_multiply_fusion), dimensions={0,1,3} | broadcast | bytes 7077888 | tf_op jit(solution)/shard_map/broadcast_in_dim | solution.py:71
  205.2 10.7 %reshape.44 = bf16[3,512,1536,1]{2,1,0,3:T(8,128)(2,1)} reshape(bf16[3,256,2,1536]{3,2,1,0:T(2,128)(2,1)} %broadcast_in_dim.23) | data formatting | bytes 9437184 | tf_op jit(solution)/shard_map/mul | solution.py:71
  215.9 12.5 %bitcast_convert_fusion = bf16[5,320,1536]{2,1,0:T(8,128)(2,1)} fusion(bf16[5,320,3,512]{3,1,0,2:T(8,128)(2,1)} %bitcast.52, bf16[3,512,1536,1]{2,1,0,3:T(8,128)(2,1)} %reshape.44), kind=kOutput, calls=%fused_computation.1 | convolution fusion | flops 7552204800 | bytes 14548992 | tf_op jit(solution)/shard_map/stj,sto->jo/dot_general | solution.py:72
  228.5 11.7 %copy.24 = bf16[5,320,1536]{1,0,2:T(8,128)(2,1)} copy(bf16[5,320,1536]{2,1,0:T(8,128)(2,1)} %bitcast_convert_fusion) | data formatting | bytes 9830400
  240.2 12.8 %reshape.49 = bf16[1536,1600]{1,0:T(8,128)(2,1)} reshape(bf16[1536,5,320]{2,1,0:T(8,128)(2,1)} %bitcast.50) | data formatting | bytes 9830400
  256.9 3.2 collective-permute-done.3
  260.0 3.2 %maximum_multiply_fusion = bf16[3,258,1536]{2,1,0:T(8,128)(2,1)S(1)} fusion(bf16[3,1,1536]{2,1,0:T(2,128)(2,1)S(1)} %collective-permute-done.3, bf16[3,256,1536]{2,1,0:T(8,128)(2,1)} %all-gather.5.cloned.1.call-done, bf16[3,1,1536]{2,1,0:T(2,128)(2,1)S(1)} %collective-permute-done.2), kind=kLoop, calls=%fused_computation.18 | loop fusion | flops 9510912 | bytes 4755456 | tf_op jit(solution)/shard_map/mul | solution.py:62
  263.2 4.3 %broadcast_in_dim.22 = bf16[3,258,2,1536]{3,2,1,0:T(2,128)(2,1)} broadcast(bf16[3,258,1536]{2,1,0:T(8,128)(2,1)S(1)} %maximum_multiply_fusion), dimensions={0,1,3} | broadcast | bytes 7133184 | tf_op jit(solution)/shard_map/broadcast_in_dim | solution.py:62
  267.5 6.4 %reshape.42 = bf16[3,516,1536,1]{2,1,0,3:T(8,128)(2,1)} reshape(bf16[3,258,2,1536]{3,2,1,0:T(2,128)(2,1)} %broadcast_in_dim.22) | data formatting | bytes 9510912 | tf_op jit(solution)/shard_map/mul | solution.py:62
  273.9 14.4 %fusion.2 = f32[3,516,5,320]{3,1,2,0:T(8,128)S(1)} fusion(bf16[5,320,1536]{2,1,0:T(8,128)(2,1)} %param.7, bf16[3,516,1536,1]{2,1,0,3:T(8,128)(2,1)} %reshape.42), kind=kOutput, calls=%fused_computation.4 | convolution fusion | flops 7608729600 | bytes 19577856 | tf_op jit(solution)/shard_map/sqo,jo->sqj/dot_general | solution.py:63
  288.4 2.1 fusion.18
  293.6 8.8 %reduce-scatter.13.cloned.1.call-done = bf16[384,1600]{1,0:T(8,128)(2,1)} async-done(((bf16[1536,1600]{1,0:T(8,128)(2,1)}), bf16[384,1600]{1,0:T(8,128)(2,1)}) %reduce-scatter.13.cloned.1.call-update) | async-done | bytes 1228816
  302.4 3.3 %reshape.50 = bf16[384,5,320]{2,1,0:T(8,128)(2,1)S(1)} reshape(bf16[384,1600]{1,0:T(8,128)(2,1)} %reduce-scatter.13.cloned.1.call-done) | data formatting | bytes 2457600
  305.6 2.4 copy.25
  308.0 2.9 convert_element_type.45
  (41 shorter events, 13.7 us)
Async XLA Ops:
  7.2 59.0 %all-gather.3.cloned.1.call-start = ((), (), s32[]{:S(2)}) async-start(), calls=%async_computation.5 | async-start | bytes 1966080 | tf_op jit(solution)/shard_map/all_gather | solution.py:46
  8.9 9.8 %copy-start.3 = (s32[512]{0:T(512)S(1)}, s32[512]{0:T(512)}, u32[]{:S(2)}) copy-start(s32[512]{0:T(512)} %param.9) | copy-start | bytes 6148
  15.0 10.0 %collective-permute-start = (bf16[3,2,320]{2,1,0:T(2,128)(2,1)S(1)}, bf16[3,2,320]{2,1,0:T(2,128)(2,1)S(1)}, u32[]{:S(2)}, u32[]{:S(2)}) collective-permute-start(bf16[3,2,320]{2,1,0:T(2,128)(2,1)S(1)} %get-tuple-element.23), channel_id=1, source_target_pairs={{0,4},{4,8},{8,12},{1,5},{5,9},{9,13},{2,6},{6,10},{10,14},{3,7},{... | collective-permute-start | bytes 11528 | tf_op jit(solution)/shard_map/ppermute | solution.py:17
  17.4 7.6 %collective-permute-start.1 = (bf16[3,2,320]{2,1,0:T(2,128)(2,1)S(1)}, bf16[3,2,320]{2,1,0:T(2,128)(2,1)S(1)}, u32[]{:S(2)}, u32[]{:S(2)}) collective-permute-start(bf16[3,2,320]{2,1,0:T(2,128)(2,1)S(1)} %get-tuple-element.22), channel_id=1, source_target_pairs={{4,0},{8,4},{12,8},{5,1},{9,5},{13,9},{6,2},{10,6},{14,10},{7,3},{... | collective-permute-start | bytes 11528 | tf_op jit(solution)/shard_map/ppermute | solution.py:19
  24.9 90.7 %reduce-scatter.9.cloned.1.call-start = ((), (), s32[]{:S(2)}) async-start(), calls=%async_computation.4 | async-start | bytes 2949120 | tf_op jit(solution)/shard_map/reduce_scatter | solution.py:42
  62.8 0.7 copy-start.4
  62.8 52.8 %copy-start.2 = (s32[3,64,512]{2,1,0:T(8,128)S(1)}, s32[3,64,512]{2,1,0:T(8,128)}, u32[]{:S(2)}) copy-start(s32[3,64,512]{2,1,0:T(8,128)} %param.11) | copy-start | bytes 1179652
  62.8 84.5 %reduce-scatter.11.cloned.1.call-start = ((), (), s32[]{:S(2)}) async-start(), calls=%async_computation.7 | async-start | bytes 1966080 | tf_op jit(solution)/shard_map/reduce_scatter | solution.py:55
  115.6 2.3 copy-start.1
  119.7 79.6 %all-gather.5.cloned.1.call-start = ((), (), s32[]{:S(2)}) async-start(), calls=%async_computation.6 | async-start | bytes 2949120 | tf_op jit(solution)/shard_map/all_gather | solution.py:53
  122.5 169.4 %reduce-scatter.15.cloned.1.call-start = ((), (), s32[]{:S(2)}) async-start(), calls=%async_computation.9 | async-start | bytes 491520
  149.2 153.1 %reduce-scatter.13.cloned.1.call-start = ((), (), s32[]{:S(2)}) async-start(), calls=%async_computation.8 | async-start | bytes 6389760
  254.0 2.9 collective-permute-start.2
  255.5 4.5 %collective-permute-start.3 = (bf16[3,1,1536]{2,1,0:T(2,128)(2,1)S(1)}, bf16[3,1,1536]{2,1,0:T(2,128)(2,1)S(1)}, u32[]{:S(2)}, u32[]{:S(2)}) collective-permute-start(bf16[3,1,1536]{2,1,0:T(2,128)(2,1)S(1)} %get-tuple-element.15), channel_id=1, source_target_pairs={{4,0},{8,4},{12,8},{5,1},{9,5},{13,9},{6,2},{10,6},{14,10},{7,3},{... | collective-permute-start | bytes 27656 | tf_op jit(solution)/shard_map/ppermute | solution.py:19
  273.9 14.4 %copy-start = (f32[3,512,320]{2,1,0:T(8,128)S(1)}, f32[3,512,320]{2,1,0:T(8,128)}, u32[]{:S(2)}) copy-start(f32[3,512,320]{2,1,0:T(8,128)} %get-tuple-element.13) | copy-start | bytes 5898244
Sparse Core Ops, SparseCore 0:
  25.0 41.1 all-gather.2
  68.5 47.0 reduce-scatter.8
  119.8 27.4 reduce-scatter.10
  149.3 49.9 all-gather.4
  201.4 19.4 reduce-scatter.14
  253.1 49.2 reduce-scatter.12
where the time goes:
time: 320 us; the launch traced here: 318 us
  waiting for transfers between devices  131 us (41%)
  local copies, waits for them, and re-layouts  96.2 us (30%)
  matrix products  46.1 us (14%)
  other arithmetic  23.2 us (7%)
  between operations  14.3 us (4%)
  starting transfers between devices  6.99 us (2%)
    all_gather x1, waiting for transfers between devices, local(): slab_grad = lax.all_gather(grad_bins, 'chan', axis=1, tiled=True)  50 us
    reduce_scatter x1, waiting for transfers between devices, local(): lax.psum_scatter(pooled_part.astype(jnp.bfloat16), 'chan', scatter_dimens...  49.4 us
    unnamed x18, local copies, waits for them, and re-layouts  36.8 us
    reduce_scatter x1, waiting for transfers between devices, local(): lax.psum_scatter(track_part.astype(jnp.bfloat16), 'seq', scatter_dimensio...  16.8 us
    dot_general x1, matrix products, local(): jnp.einsum('sqo,jo->sqj', wide_grad, flat_weight, preferred_element_type=...  14.4 us
    dot_general x1, matrix products, local(): jnp.einsum('stj,sto->jo', windows, slab_upsampled, preferred_element_type...  12.5 us
    dot_general x1, matrix products, local(): jnp.einsum('stj,jo->sto', windows, flat_weight, preferred_element_type=jn...  12.4 us
    dot_general x1, local copies, waits for them, and re-layouts, local(): jnp.einsum('stj,jo->sto', windows, flat_weight, preferred_element_type=jn...  11 us
  transfers between devices with their start and end apart: 10, of which 6 were waited for; matrix products, arithmetic and copies ran while one was open for 46% of the time, Pallas kernels for 0%

commit v1 on v0

--- a/solution.py
+++ b/solution.py
@@ -2,8 +2,18 @@
 import jax.numpy as jnp
 from jax import lax
 from jax.sharding import PartitionSpec as P
+from jax.lax import axis_index, axis_size, ppermute
 
 KSIZE = 5
+
+
+def set_spots_in(array_in, axis_no):
+    array_in = jnp.moveaxis(array_in, 0, axis_no)
+    known = array_in.shape
+    current_block = array_in.reshape(
+        *known[:axis_no], known[axis_no] * known[axis_no + 1], *known[axis_no + 2 :]
+    )
+    return current_block
 
 
 def padded_2(cells, sides, width):
@@ -50,7 +60,19 @@
     grad_bins = jnp.einsum(
         "snm,md->snd", grad_logit, chosen, preferred_element_type=jnp.float32
     ).astype(jnp.bfloat16)
-    slab_grad = lax.all_gather(grad_bins, "chan", axis=1, tiled=True)
+    q_n = axis_size("chan")
+    gallery = tuple(((m, (m + 1) % q_n) for m in range(q_n)))
+    bank = tuple(((j0, c) for c, j0 in gallery))
+    v1, a_now = ([], [])
+    for to_i in [*range(q_n - 1)]:
+        if to_i % 2 == 0:
+            v1.append(ppermute(v1[-1] if v1 else grad_bins, "chan", perm=gallery))
+        else:
+            a_now.append(ppermute(a_now[-1] if a_now else grad_bins, perm=bank, axis_name="chan"))
+    wide_out = jnp.stack([*v1[::-1], grad_bins, *a_now], axis=0)
+    carry = axis_index("chan") - len(v1)
+    wide_out = wide_out[(jnp.arange(q_n) - carry) % q_n]
+    slab_grad = set_spots_in(wide_out, 1)
     track_part = jnp.einsum("snm,snd->md", grad_logit, bin_rows, preferred_element_type=jnp.float32)
     track_summed = lax.psum_scatter(
         track_part.astype(jnp.bfloat16), "seq", scatter_dimension=0, tiled=True

time: 320 us -> 287 us (0.90)
  waiting for transfers between devices: 131 us -> 95.3 us
  starting transfers between devices: 6.99 us -> 11 us
    all_gather x1 -> x0, waiting for transfers between devices: 50 us -> none  [local(): slab_grad = lax.all_gather(grad_bins, 'chan', axis=1, tiled=True)]
    ppermute x0 -> x3, waiting for transfers between devices: none -> 30.1 us  [the longest x2 27.4 us: local(): v1.append(ppermute(v1[-1] if v1 else grad_bins, 'chan', perm=gallery))]
    reduce_scatter x1, waiting for transfers between devices: 16.8 us -> 0.01 us  [local(): lax.psum_scatter(track_part.astype(jnp.bfloat16), 'seq', scatter_dimensio...]
    ppermute x0 -> x3, starting transfers between devices: none -> 3.88 us  [the longest x1 3 us: local(): ppermute(a_now[-1] if a_now else grad_bins, perm=bank, axis_name='chan')]
    unnamed x8 -> x7, waiting for transfers between devices: 8.85 us -> 11.4 us
    unnamed x18 -> x26, local copies, waits for them, and re-layouts: 36.8 us -> 36.8 us
  transfers between devices with their start and end apart: 10 -> 12, of which waited for: 6 -> 7; matrix products, arithmetic and copies ran while one was open for 46% -> 50% of each run, Pallas kernels for 0% -> 0%
where the time goes in v1:
time: 287 us; the launch traced here: 285 us
  local copies, waits for them, and re-layouts  99.3 us (35%)
  waiting for transfers between devices  95.3 us (33%)
  matrix products  44.5 us (16%)
  other arithmetic  21.1 us (7%)
  between operations  14 us (5%)
  starting transfers between devices  11 us (4%)
    reduce_scatter x1, waiting for transfers between devices, local(): lax.psum_scatter(pooled_part.astype(jnp.bfloat16), 'chan', scatter_dimens...  49.4 us
    unnamed x26, local copies, waits for them, and re-layouts  36.8 us
    ppermute x2, waiting for transfers between devices, local(): v1.append(ppermute(v1[-1] if v1 else grad_bins, 'chan', perm=gallery))  27.4 us
    dot_general x1, matrix products, local(): jnp.einsum('sqo,jo->sqj', wide_grad, flat_weight, preferred_element_type=...  14.9 us
    dot_general x1, matrix products, local(): jnp.einsum('stj,sto->jo', windows, slab_upsampled, preferred_element_type...  12.6 us
    dot_general x1, matrix products, local(): jnp.einsum('stj,jo->sto', windows, flat_weight, preferred_element_type=jn...  12.4 us
    unnamed x7, waiting for transfers between devices  11.4 us
    dot_general x1, local copies, waits for them, and re-layouts, local(): jnp.einsum('stj,jo->sto', windows, flat_weight, preferred_element_type=jn...  10.9 us
  transfers between devices with their start and end apart: 12, of which 7 were waited for; matrix products, arithmetic and copies ran while one was open for 50% of the time, Pallas kernels for 0%

profile of v1, /device:TPU:0, one launch (start us, length us, event | category | flops | bytes accessed | tf_op | source)
XLA Modules:
  0.0 285.2 jit_solution(9246368447598740054)
XLA Ops:
  8.9 6.0 %fusion.12 = (bf16[3,512,320]{2,1,0:T(8,128)(2,1)S(1)}, f32[3,512,320]{2,1,0:T(8,128)}) fusion(bf16[3,512,320]{2,1,0:T(8,128)(2,1)S(1)} %copy.18), kind=kLoop, calls=%fused_computation.20 | loop fusion | flops 32440320 | bytes 3932160 | tf_op jit(solution)/shard_map/convert_element_type | solution.py:44
  16.3 3.0 %collective-permute-start = (bf16[3,2,320]{2,1,0:T(2,128)(2,1)S(1)}, bf16[3,2,320]{2,1,0:T(2,128)(2,1)S(1)}, u32[]{:S(2)}, u32[]{:S(2)}) collective-permute-start(bf16[3,2,320]{2,1,0:T(2,128)(2,1)S(1)} %get-tuple-element.23), channel_id=1, source_target_pairs={{0,4},{4,8},{8,12},{1,5},{5,9},{9,13},{2,6},{6,10},{10,14},{3,7},{... | collective-permute-start | bytes 11528 | tf_op jit(solution)/shard_map/ppermute | solution.py:27
  19.3 5.2 %gather_fusion = bf16[512,384]{1,0:T(8,128)(2,1)S(1)} fusion(bf16[7611,384]{1,0:T(8,128)(2,1)} %param.8, s32[1024]{0:T(1024)S(1)} %pad_clamp_fusion.1), kind=kCustom, calls=%fused_computation | custom fusion | bytes 788480 | tf_op jit(solution)/shard_map/jit(_take)/gather | solution.py:55
  25.6 3.4 %pad_maximum_fusion.1 = (bf16[3,512,320]{2,1,0:T(8,128)(2,1)S(1)}, bf16[3,512,320]{2,1,0:T(8,128)(2,1)}, bf16[3,512,320]{2,1,0:T(8,128)(2,1)}, bf16[3,512,320]{2,1,0:T(8,128)(2,1)}) fusion(bf16[3,2,320]{2,1,0:T(2,128)(2,1)S(1)} %collective-permute-done.1, bf16[3,512,320]{2,1,0:T(8,128)(2,1)S(1)} %get-tuple-element.12, ...), kind=kLoop, calls=%fused_computation.73 | loop fusion | flops 7864320 | bytes 4922880 | tf_op jit(solution)/shard_map/concatenate | solution.py:25
  28.9 9.0 %concatenate.17 = bf16[3,512,1600]{2,1,0:T(8,128)(2,1)} concatenate(bf16[3,512,320]{2,1,0:T(8,128)(2,1)} %get-tuple-element.20, bf16[3,512,320]{2,1,0:T(8,128)(2,1)} %get-tuple-element.21, bf16[3,512,320]{2,1,0:T(8,128)(2,1)S(1)} %get-tuple-element.12, bf16[3,512,320]{2,1,0:T(8,128)(2,1)} %get-tuple-element.17, bf16[3,512,320]{2,1,0:T(8,128)(2,1)S(1)} %get-tuple-element.16), dimensions={2} | concatenate | bytes 9830400 | tf_op jit(solution)/shard_map/concatenate | solution.py:46
  37.9 10.9 %dot_general.24 = bf16[3,256,2,1600]{3,2,1,0:T(2,128)(2,1)} reshape(bf16[3,512,1600]{2,1,0:T(8,128)(2,1)} %concatenate.17) | data formatting | bytes 9830400 | tf_op jit(solution)/shard_map/stj,jo->sto/dot_general | solution.py:50
  48.8 12.4 %fusion.7 = f32[3,256,1536]{2,1,0:T(8,128)S(1)} fusion(bf16[1600,1536,1,1]{1,0,3,2:T(8,128)(2,1)} %bitcast.70, bf16[3,256,2,1600]{3,2,1,0:T(2,128)(2,1)} %dot_general.24), kind=kOutput, calls=%fused_computation.15 | convolution fusion | flops 7550926848 | bytes 14548992 | tf_op jit(solution)/shard_map/stj,jo->sto/dot_general | solution.py:50
  61.2 2.0 multiply_convert_fusion
  65.0 49.4 %reduce-scatter.9.cloned.1.call-done = bf16[3,64,1536]{2,1,0:T(8,128)(2,1)} async-done(((bf16[3,256,1536]{2,1,0:T(8,128)(2,1)}), bf16[3,64,1536]{2,1,0:T(8,128)(2,1)}) %reduce-scatter.9.cloned.1.call-update) | async-done | bytes 589840 | tf_op jit(solution)/shard_map/reduce_scatter | solution.py:52
  114.3 2.3 fusion.62
  119.9 3.0 %collective-permute-start.4 = (bf16[3,64,1536]{2,1,0:T(8,128)(2,1)S(1)}, bf16[3,64,1536]{2,1,0:T(8,128)(2,1)S(1)}, u32[]{:S(2)}, u32[]{:S(2)}) collective-permute-start(bf16[3,64,1536]{2,1,0:T(8,128)(2,1)S(1)} %convolution_convert_fusion), channel_id=1, source_target_pairs={{1,0},{2,1},{3,2},{0,3},{5,4},{6,5},{7,6},{4,7},{9,8},{10,9},{11,1... | collective-permute-start | bytes 1769480 | tf_op jit(solution)/shard_map/ppermute | solution.py:71
  122.9 14.2 %collective-permute-done.2 = bf16[3,64,1536]{2,1,0:T(8,128)(2,1)S(1)} collective-permute-done((bf16[3,64,1536]{2,1,0:T(8,128)(2,1)S(1)}, bf16[3,64,1536]{2,1,0:T(8,128)(2,1)S(1)}, u32[]{:S(2)}, u32[]{:S(2)}) %collective-permute-start.2) | collective-permute-done | bytes 589856 | tf_op jit(solution)/shard_map/ppermute | solution.py:69
  137.2 7.9 %copy.21 = bf16[1600,3,512]{2,0,1:T(8,128)(2,1)} copy(bf16[1600,3,512]{0,2,1:T(8,128)(2,1)} %bitcast.58) | data formatting | bytes 9830400 | tf_op jit(solution)/shard_map/stj,sto->jo/dot_general | solution.py:94
  145.1 2.7 collective-permute-done.4
  147.8 13.2 %collective-permute-done.3 = bf16[3,64,1536]{2,1,0:T(8,128)(2,1)} collective-permute-done((bf16[3,64,1536]{2,1,0:T(8,128)(2,1)S(1)}, bf16[3,64,1536]{2,1,0:T(8,128)(2,1)}, u32[]{:S(2)}, u32[]{:S(2)}) %collective-permute-start.3) | collective-permute-done | bytes 589856 | tf_op jit(solution)/shard_map/ppermute | solution.py:69
  162.9 2.1 gather_fusion.1
  165.0 1.9 copy.20
  167.3 4.0 %broadcast_in_dim.24 = bf16[3,256,2,1536]{3,2,1,0:T(2,128)(2,1)} broadcast(bf16[3,256,1536]{2,1,0:T(8,128)(2,1)S(1)} %broadcast_multiply_fusion), dimensions={0,1,3} | broadcast | bytes 7077888 | tf_op jit(solution)/shard_map/broadcast_in_dim | solution.py:93
  171.3 10.7 %reshape.105 = bf16[3,512,1536,1]{2,1,0,3:T(8,128)(2,1)} reshape(bf16[3,256,2,1536]{3,2,1,0:T(2,128)(2,1)} %broadcast_in_dim.24) | data formatting | bytes 9437184 | tf_op jit(solution)/shard_map/mul | solution.py:93
  182.0 1.9 copy.28
  184.0 12.6 %bitcast_convert_fusion = bf16[5,320,1536]{2,1,0:T(8,128)(2,1)} fusion(bf16[5,320,3,512]{3,1,0,2:T(8,128)(2,1)} %bitcast.64, bf16[3,512,1536,1]{2,1,0,3:T(8,128)(2,1)} %reshape.105), kind=kOutput, calls=%fused_computation.2 | convolution fusion | flops 7552204800 | bytes 14548992 | tf_op jit(solution)/shard_map/stj,sto->jo/dot_general | solution.py:94
  196.5 11.7 %copy.26 = bf16[5,320,1536]{1,0,2:T(8,128)(2,1)} copy(bf16[5,320,1536]{2,1,0:T(8,128)(2,1)} %bitcast_convert_fusion) | data formatting | bytes 9830400
  208.3 12.8 %reshape.110 = bf16[1536,1600]{1,0:T(8,128)(2,1)} reshape(bf16[1536,5,320]{2,1,0:T(8,128)(2,1)} %bitcast.59) | data formatting | bytes 9830400
  223.7 3.5 %collective-permute-done.6 = bf16[3,1,1536]{2,1,0:T(2,128)(2,1)S(1)} collective-permute-done((bf16[3,1,1536]{2,1,0:T(2,128)(2,1)S(1)}, bf16[3,1,1536]{2,1,0:T(2,128)(2,1)S(1)}, u32[]{:S(2)}, u32[]{:S(2)}) %collective-permute-start.6) | collective-permute-done | bytes 9248 | tf_op jit(solution)/shard_map/ppermute | solution.py:29
  228.0 4.3 %broadcast_in_dim.23 = bf16[3,258,2,1536]{3,2,1,0:T(2,128)(2,1)} broadcast(bf16[3,258,1536]{2,1,0:T(8,128)(2,1)S(1)} %maximum_multiply_fusion), dimensions={0,1,3} | broadcast | bytes 7133184 | tf_op jit(solution)/shard_map/broadcast_in_dim | solution.py:84
  232.2 6.3 %reshape.103 = bf16[3,516,1536,1]{2,1,0,3:T(8,128)(2,1)} reshape(bf16[3,258,2,1536]{3,2,1,0:T(2,128)(2,1)} %broadcast_in_dim.23) | data formatting | bytes 9510912 | tf_op jit(solution)/shard_map/mul | solution.py:84
  238.6 14.9 %fusion.2 = f32[3,516,5,320]{3,1,2,0:T(8,128)S(1)} fusion(bf16[5,320,1536]{2,1,0:T(8,128)(2,1)} %param.7, bf16[3,516,1536,1]{2,1,0,3:T(8,128)(2,1)} %reshape.103), kind=kOutput, calls=%fused_computation.5 | convolution fusion | flops 7608729600 | bytes 19577856 | tf_op jit(solution)/shard_map/sqo,jo->sqj/dot_general | solution.py:85
  253.6 2.1 fusion.18
  258.8 11.3 %reduce-scatter.13.cloned.1.call-done = bf16[384,1600]{1,0:T(8,128)(2,1)} async-done(((bf16[1536,1600]{1,0:T(8,128)(2,1)}), bf16[384,1600]{1,0:T(8,128)(2,1)}) %reduce-scatter.13.cloned.1.call-update) | async-done | bytes 1228816
  270.1 3.3 %reshape.111 = bf16[384,5,320]{2,1,0:T(8,128)(2,1)S(1)} reshape(bf16[384,1600]{1,0:T(8,128)(2,1)} %reduce-scatter.13.cloned.1.call-done) | data formatting | bytes 2457600
  273.3 2.4 copy.27
  275.8 2.9 %convert_element_type.45 = f32[5,320,384]{2,1,0:T(8,128)} convert(bf16[5,320,384]{2,1,0:T(8,128)(2,1)} %copy.27) | non-fusion elementwise | flops 614400 | bytes 3686400 | tf_op jit(solution)/shard_map/convert_element_type | solution.py:102
  (57 shorter events, 17.7 us)
Async XLA Ops:
  7.2 57.8 %all-gather.2.cloned.1.call-start = ((), (), s32[]{:S(2)}) async-start(), calls=%async_computation.5 | async-start | bytes 1966080 | tf_op jit(solution)/shard_map/all_gather | solution.py:56
  8.9 10.4 %copy-start.7 = (s32[512]{0:T(512)S(1)}, s32[512]{0:T(512)}, u32[]{:S(2)}) copy-start(s32[512]{0:T(512)} %param.9) | copy-start | bytes 6148
  15.0 10.6 %collective-permute-start.1 = (bf16[3,2,320]{2,1,0:T(2,128)(2,1)S(1)}, bf16[3,2,320]{2,1,0:T(2,128)(2,1)S(1)}, u32[]{:S(2)}, u32[]{:S(2)}) collective-permute-start(bf16[3,2,320]{2,1,0:T(2,128)(2,1)S(1)} %get-tuple-element.22), channel_id=1, source_target_pairs={{4,0},{8,4},{12,8},{5,1},{9,5},{13,9},{6,2},{10,6},{14,10},{7,3},{... | collective-permute-start | bytes 11528 | tf_op jit(solution)/shard_map/ppermute | solution.py:29
  16.3 9.3 %collective-permute-start = (bf16[3,2,320]{2,1,0:T(2,128)(2,1)S(1)}, bf16[3,2,320]{2,1,0:T(2,128)(2,1)S(1)}, u32[]{:S(2)}, u32[]{:S(2)}) collective-permute-start(bf16[3,2,320]{2,1,0:T(2,128)(2,1)S(1)} %get-tuple-element.23), channel_id=1, source_target_pairs={{0,4},{4,8},{8,12},{1,5},{5,9},{9,13},{2,6},{6,10},{10,14},{3,7},{... | collective-permute-start | bytes 11528 | tf_op jit(solution)/shard_map/ppermute | solution.py:27
  25.5 88.9 %reduce-scatter.9.cloned.1.call-start = ((), (), s32[]{:S(2)}) async-start(), calls=%async_computation.4 | async-start | bytes 2949120 | tf_op jit(solution)/shard_map/reduce_scatter | solution.py:52
  63.3 0.7 copy-start.8
  63.3 51.1 %copy-start.6 = (s32[3,64,512]{2,1,0:T(8,128)S(1)}, s32[3,64,512]{2,1,0:T(8,128)}, u32[]{:S(2)}) copy-start(s32[3,64,512]{2,1,0:T(8,128)} %param.11) | copy-start | bytes 1179652
  63.3 118.7 %reduce-scatter.11.cloned.1.call-start = ((), (), s32[]{:S(2)}) async-start(), calls=%async_computation.6 | async-start | bytes 1966080 | tf_op jit(solution)/shard_map/reduce_scatter | solution.py:77
  114.3 2.3 copy-start.5
  116.7 1.8 copy-start.1
  118.5 138.6 %reduce-scatter.15.cloned.1.call-start = ((), (), s32[]{:S(2)}) async-start(), calls=%async_computation.8 | async-start | bytes 491520
  119.0 26.1 %copy-start.2 = (bf16[3,64,1536]{2,1,0:T(8,128)(2,1)}, bf16[3,64,1536]{2,1,0:T(8,128)(2,1)S(1)}, u32[]{:S(2)}) copy-start(bf16[3,64,1536]{2,1,0:T(8,128)(2,1)S(1)} %convolution_convert_fusion) | copy-start | bytes 1769476
  119.1 18.1 %collective-permute-start.2 = (bf16[3,64,1536]{2,1,0:T(8,128)(2,1)S(1)}, bf16[3,64,1536]{2,1,0:T(8,128)(2,1)S(1)}, u32[]{:S(2)}, u32[]{:S(2)}) collective-permute-start(bf16[3,64,1536]{2,1,0:T(8,128)(2,1)S(1)} %convolution_convert_fusion), channel_id=1, source_target_pairs={{0,1},{1,2},{2,3},{3,0},{4,5},{5,6},{6,7},{7,4},{8,9},{9,10},{10,1... | collective-permute-start | bytes 1769480 | tf_op jit(solution)/shard_map/ppermute | solution.py:69
  119.9 27.9 %collective-permute-start.4 = (bf16[3,64,1536]{2,1,0:T(8,128)(2,1)S(1)}, bf16[3,64,1536]{2,1,0:T(8,128)(2,1)S(1)}, u32[]{:S(2)}, u32[]{:S(2)}) collective-permute-start(bf16[3,64,1536]{2,1,0:T(8,128)(2,1)S(1)} %convolution_convert_fusion), channel_id=1, source_target_pairs={{1,0},{2,1},{3,2},{0,3},{5,4},{6,5},{7,6},{4,7},{9,8},{10,9},{11,1... | collective-permute-start | bytes 1769480 | tf_op jit(solution)/shard_map/ppermute | solution.py:71
  137.2 8.0 %copy-start.3 = (bf16[3,64,1536]{2,1,0:T(8,128)(2,1)}, bf16[3,64,1536]{2,1,0:T(8,128)(2,1)S(1)}, u32[]{:S(2)}) copy-start(bf16[3,64,1536]{2,1,0:T(8,128)(2,1)S(1)} %collective-permute-done.2) | copy-start | bytes 1769476
  137.2 23.8 %collective-permute-start.3 = (bf16[3,64,1536]{2,1,0:T(8,128)(2,1)S(1)}, bf16[3,64,1536]{2,1,0:T(8,128)(2,1)}, u32[]{:S(2)}, u32[]{:S(2)}) collective-permute-start(bf16[3,64,1536]{2,1,0:T(8,128)(2,1)S(1)} %collective-permute-done.2), channel_id=1, source_target_pairs={{0,1},{1,2},{2,3},{3,0},{4,5},{5,6},{6,7},{7,4},{8,9},{9,10},{10,1... | collective-permute-start | bytes 1769480 | tf_op jit(solution)/shard_map/ppermute | solution.py:69
  147.8 13.2 %copy-start.4 = (bf16[3,64,1536]{2,1,0:T(8,128)(2,1)}, bf16[3,64,1536]{2,1,0:T(8,128)(2,1)S(1)}, u32[]{:S(2)}) copy-start(bf16[3,64,1536]{2,1,0:T(8,128)(2,1)S(1)} %collective-permute-done.4) | copy-start | bytes 1769476
  183.9 86.2 %reduce-scatter.13.cloned.1.call-start = ((), (), s32[]{:S(2)}) async-start(), calls=%async_computation.7 | async-start | bytes 6389760
  221.1 2.6 collective-permute-start.5
  222.4 4.8 %collective-permute-start.6 = (bf16[3,1,1536]{2,1,0:T(2,128)(2,1)S(1)}, bf16[3,1,1536]{2,1,0:T(2,128)(2,1)S(1)}, u32[]{:S(2)}, u32[]{:S(2)}) collective-permute-start(bf16[3,1,1536]{2,1,0:T(2,128)(2,1)S(1)} %get-tuple-element.15), channel_id=1, source_target_pairs={{4,0},{8,4},{12,8},{5,1},{9,5},{13,9},{6,2},{10,6},{14,10},{7,3},{... | collective-permute-start | bytes 27656 | tf_op jit(solution)/shard_map/ppermute | solution.py:29
  238.6 14.9 %copy-start = (f32[3,512,320]{2,1,0:T(8,128)S(1)}, f32[3,512,320]{2,1,0:T(8,128)}, u32[]{:S(2)}) copy-start(f32[3,512,320]{2,1,0:T(8,128)} %get-tuple-element.13) | copy-start | bytes 5898244
Sparse Core Ops, SparseCore 0:
  25.6 39.3 all-gather.1
  67.3 47.0 reduce-scatter.8
  118.6 27.4 reduce-scatter.10
  184.0 19.0 reduce-scatter.14
  221.2 48.8 reduce-scatter.12
